TPU v7x, 32 devices: a whole 2x2x4 slice. The times are simulated.
32 devices in a mesh: fsdp: 4 (over x, core), ctx: 4 (over z), tp: 2 (over y).
Axes of the slice: x: 2, y: 2, z: 4, core: 2. Of those that a mesh axis runs over, the one named last changes fastest.
Arguments:
- tokens: bfloat16 [8, 4096, 768], P('fsdp', 'ctx'), may hold values from -6 to 6
- qkv_weight: bfloat16 [768, 3, 768], P(('fsdp', 'ctx'), None, 'tp'), may hold values from -0.21875 to 0.21875
- qv_bias: bfloat16 [2, 768], P(None, 'tp'), may hold values from -3 to 3
- out_weight: bfloat16 [768, 768], P(('fsdp', 'ctx'), 'tp'), may hold values from -8 to 8
- up_weight: bfloat16 [768, 3072], P(('fsdp', 'ctx'), 'tp'), may hold values from -0.21875 to 0.21875
- up_bias: bfloat16 [3072], P('tp'), may hold values from -3 to 3
- down_weight: bfloat16 [768, 3072], P(('fsdp', 'ctx'), 'tp'), may hold values from -0.109375 to 0.109375
- norm_gains: bfloat16 [768, 2], P(('fsdp', 'ctx')), may hold values from 0.5 to 1.5
- row_biases: bfloat16 [768, 4], P(('fsdp', 'ctx')), may hold values from -3 to 3
- cotangent: bfloat16 [8, 4096, 768], P('fsdp', 'ctx'), may hold values from -6 to 6
Outputs:
- output: bfloat16 [8, 4096, 768], P('fsdp', ('ctx', 'tp'))
- tokens_grad: bfloat16 [8, 4096, 768], P('fsdp', ('ctx', 'tp'))
- qkv_weight_grad: float32 [768, 3, 768], P(('fsdp', 'ctx'), None, 'tp')
- qv_bias_grad: float32 [2, 768], P(None, 'tp')
- out_weight_grad: float32 [768, 768], P(('fsdp', 'ctx'), 'tp')
- up_weight_grad: float32 [768, 3072], P(('fsdp', 'ctx'), 'tp')
- up_bias_grad: float32 [3072], P('tp')
- down_weight_grad: float32 [768, 3072], P(('fsdp', 'ctx'), 'tp')
- norm_gains_grad: float32 [768, 2], P(('fsdp', 'ctx'))
- row_biases_grad: float32 [768, 4], P(('fsdp', 'ctx'))
All inputs are finite; a program needn't handle non-finite values.
Results may differ from a plain program's by a relative error of at most 0.02.
Values may be sent and summed in bfloat16 or wider, within the bound.
No kernel may reach another device: no remote copies, remote signals or barrier semaphores. Data moves between devices by JAX's collectives and lax.ppermute only.
A program may use at most 256 MiB of HBM per device.

v0:
```python
import jax
import jax.numpy as jnp
from jax import lax
from jax.sharding import PartitionSpec as P

HD = 64
epsilon = 1e-12
score_scale = 0.125
highest = lax.Precision.HIGHEST


def contract_last(left, right):
    return lax.dot_general(
        left, right, (((1,), (1,)), ((), ())), preferred_element_type=jnp.float32
    )


def contract_first(left, right):
    return lax.dot_general(
        left, right, (((0,), (0,)), ((), ())), preferred_element_type=jnp.float32
    )


def norm_forward(hidden, gain, shift):
    center = hidden - jnp.mean(hidden, axis=-1, keepdims=True)
    inv_scale = lax.rsqrt(jnp.mean(center * center, axis=-1, keepdims=True) + epsilon)
    normed = center * inv_scale
    return (normed * gain + shift, normed, inv_scale)


def norm_backward(grad_out, normed, inv_scale, gain):
    grad_norm = grad_out * gain
    return inv_scale * (
        grad_norm
        - jnp.mean(grad_norm, axis=-1, keepdims=True)
        - normed * jnp.mean(grad_norm * normed, axis=-1, keepdims=True)
    )


def gelu_exact(values):
    return jax.nn.gelu(values, approximate=False)


def split_heads(array, first_row, row_count, head_count):
    piece = lax.dynamic_slice_in_dim(array, first_row, row_count, 1)
    return piece.reshape(piece.shape[0], row_count, head_count, piece.shape[2] // head_count)


def block_scores(query_four, key_four):
    return (
        jnp.einsum("sqhd,skhd->shqk", query_four, key_four, preferred_element_type=jnp.float32)
        * score_scale
    )


def softmax_rows(scores, row_max, row_total):
    return jnp.exp(scores - row_max[..., None]) / row_total[..., None]


def score_grads(scores, row_max, row_total, row_delta, grad_four, value_four):
    prob_full = softmax_rows(scores, row_max, row_total)
    prob_grad = jnp.einsum(
        "sqhd,skhd->shqk", grad_four, value_four, preferred_element_type=jnp.float32
    )
    score_low = (prob_full * (prob_grad - row_delta[..., None])).astype(jnp.bfloat16)
    return (prob_full.astype(jnp.bfloat16), score_low)


def body(
    tokens,
    qkv_weight,
    qv_bias,
    out_weight,
    up_weight,
    up_bias,
    down_weight,
    norm_gains,
    row_biases,
    cotangent,
):
    seq_count, local_len, width = tokens.shape
    row_count = seq_count * local_len
    tp_count = lax.axis_size("tp")
    share_len = local_len // tp_count
    share_start = lax.axis_index("tp") * share_len

    def own_rows(array_three):
        return lax.dynamic_slice_in_dim(array_three, share_start, share_len, 1)

    def to_three(array_two):
        return array_two.reshape(seq_count, array_two.shape[0] // seq_count, array_two.shape[1])

    gathered = (
        lax.all_gather(qkv_weight, ("fsdp", "ctx"), axis=0, tiled=True),
        lax.all_gather(out_weight, ("fsdp", "ctx"), axis=0, tiled=True),
        lax.all_gather(up_weight, ("fsdp", "ctx"), axis=0, tiled=True),
        lax.all_gather(down_weight, ("fsdp", "ctx"), axis=0, tiled=True),
        lax.all_gather(norm_gains, ("fsdp", "ctx"), axis=0, tiled=True),
        lax.all_gather(row_biases, ("fsdp", "ctx"), axis=0, tiled=True),
    )
    w_qkv, w_out, w_up, w_down, gains_all, biases_all = gathered
    gains_f = gains_all.astype(jnp.float32)
    biases_f = biases_all.astype(jnp.float32)
    head_width = w_qkv.shape[2]
    head_count = head_width // HD
    flat_tokens = tokens.reshape(row_count, width)
    projected = jnp.dot(
        flat_tokens, w_qkv.reshape(width, 3 * head_width), preferred_element_type=jnp.float32
    )
    projected = projected.reshape(row_count, 3, head_width)
    bias_f = qv_bias.astype(jnp.float32)
    query_low = (projected[:, 0] + bias_f[0]).astype(jnp.bfloat16)
    key_low = projected[:, 1].astype(jnp.bfloat16)
    value_low = (projected[:, 2] + bias_f[1]).astype(jnp.bfloat16)
    keys_full, values_full = (
        lax.all_gather(
            key_low.reshape(seq_count, local_len, head_width), "ctx", axis=1, tiled=True
        ),
        lax.all_gather(
            value_low.reshape(seq_count, local_len, head_width), "ctx", axis=1, tiled=True
        ),
    )
    full_len = keys_full.shape[1]
    block_len = min(512, full_len)
    block_count = full_len // block_len
    query_four = query_low.reshape(seq_count, local_len, head_count, HD)
    stat_shape = (seq_count, head_count, local_len)
    four_shape = (seq_count, local_len, head_count, HD)

    def stats_step(block_idx, running):
        row_max, row_total = running
        scores = block_scores(
            query_four, split_heads(keys_full, block_idx * block_len, block_len, head_count)
        )
        new_max = jnp.maximum(row_max, jnp.max(scores, axis=-1))
        row_total = row_total * jnp.exp(row_max - new_max) + jnp.sum(
            jnp.exp(scores - new_max[..., None]), axis=-1
        )
        return (new_max, row_total)

    row_max, row_total = lax.fori_loop(
        0,
        block_count,
        stats_step,
        (jnp.full(stat_shape, -jnp.inf, jnp.float32), jnp.zeros(stat_shape, jnp.float32)),
    )

    def value_step(block_idx, attn_mixed):
        first_row = block_idx * block_len
        value_four = split_heads(values_full, first_row, block_len, head_count)
        prob_full = softmax_rows(
            block_scores(query_four, split_heads(keys_full, first_row, block_len, head_count)),
            row_max,
            row_total,
        )
        return attn_mixed + jnp.einsum(
            "shqk,skhd->sqhd",
            prob_full.astype(jnp.bfloat16),
            value_four,
            preferred_element_type=jnp.float32,
        )

    zero_four = jnp.zeros(four_shape, jnp.float32)
    attn_mixed = lax.fori_loop(0, block_count, value_step, zero_four)
    mixed_low = attn_mixed.reshape(row_count, head_width).astype(jnp.bfloat16)
    attn_part = contract_last(mixed_low, w_out)
    attn_out = lax.psum(attn_part.astype(jnp.bfloat16), "tp").astype(jnp.float32) + biases_f[:, 0]
    first_out, first_norm, first_scale = norm_forward(
        flat_tokens.astype(jnp.float32) + attn_out, gains_f[:, 0], biases_f[:, 1]
    )
    first_low = first_out.astype(jnp.bfloat16)
    inner_pre = jnp.dot(first_low, w_up, preferred_element_type=jnp.float32) + up_bias.astype(
        jnp.float32
    )
    activated, gelu_back = jax.vjp(gelu_exact, inner_pre)
    act_low = activated.astype(jnp.bfloat16)
    ffn_part = contract_last(act_low, w_down)
    ffn_out = lax.psum(ffn_part.astype(jnp.bfloat16), "tp").astype(jnp.float32) + biases_f[:, 2]
    grad_final = cotangent.reshape(row_count, width).astype(jnp.float32)
    final_out, final_norm, final_scale = norm_forward(
        first_out + ffn_out, gains_f[:, 1], biases_f[:, 3]
    )
    gain2_grad = jnp.sum(grad_final * final_norm, axis=0)
    shift2_grad = jnp.sum(grad_final, axis=0)
    grad_second = norm_backward(grad_final, final_norm, final_scale, gains_f[:, 1])
    ffn_grad_low = grad_second.astype(jnp.bfloat16)
    down_grad = contract_first(ffn_grad_low, act_low)
    down_bias_grad = jnp.sum(ffn_grad_low.astype(jnp.float32), axis=0)
    act_grad = jnp.dot(ffn_grad_low, w_down, preferred_element_type=jnp.float32)
    inner_low = gelu_back(act_grad)[0].astype(jnp.bfloat16)
    up_grad = contract_first(first_low, inner_low)
    up_bias_grad = jnp.sum(inner_low.astype(jnp.float32), axis=0)
    back_part = contract_last(inner_low, w_up)
    first_grad = grad_second + lax.psum(back_part.astype(jnp.bfloat16), "tp").astype(jnp.float32)
    gain1_grad = jnp.sum(first_grad * first_norm, axis=0)
    shift1_grad = jnp.sum(first_grad, axis=0)
    resid_grad = norm_backward(first_grad, first_norm, first_scale, gains_f[:, 0])
    attn_grad_low = resid_grad.astype(jnp.bfloat16)
    out_grad = contract_first(attn_grad_low, mixed_low)
    out_bias_grad = jnp.sum(attn_grad_low.astype(jnp.float32), axis=0)
    mixed_grad_low = jnp.dot(attn_grad_low, w_out, preferred_element_type=jnp.float32).astype(
        jnp.bfloat16
    )
    grad_four = mixed_grad_low.reshape(four_shape)
    row_delta = jnp.einsum(
        "sqhd,sqhd->shq", grad_four.astype(jnp.float32), attn_mixed, precision=highest
    )

    def grad_step(block_idx, running):
        query_grad, key_all, value_all = running
        first_row = block_idx * block_len
        key_four = split_heads(keys_full, first_row, block_len, head_count)
        value_four = split_heads(values_full, first_row, block_len, head_count)
        scores = block_scores(query_four, key_four)
        prob_low, score_low = score_grads(
            scores, row_max, row_total, row_delta, grad_four, value_four
        )
        query_grad = query_grad + jnp.einsum(
            "shqk,skhd->sqhd", score_low, key_four, preferred_element_type=jnp.float32
        )
        key_part = (
            jnp.einsum("shqk,sqhd->skhd", score_low, query_four, preferred_element_type=jnp.float32)
            * score_scale
        )
        value_part = jnp.einsum(
            "shqk,sqhd->skhd", prob_low, grad_four, preferred_element_type=jnp.float32
        )
        key_all = lax.dynamic_update_slice_in_dim(
            key_all, key_part.reshape(seq_count, block_len, head_width), first_row, 1
        )
        value_all = lax.dynamic_update_slice_in_dim(
            value_all, value_part.reshape(seq_count, block_len, head_width), first_row, 1
        )
        return (query_grad, key_all, value_all)

    zeros_full = jnp.zeros((seq_count, full_len, head_width), jnp.float32)
    query_grad, key_all, value_all = lax.fori_loop(
        0, block_count, grad_step, (zero_four, zeros_full, zeros_full)
    )
    key_grad, value_grad = (
        lax.psum_scatter(
            key_all.astype(jnp.bfloat16), "ctx", scatter_dimension=1, tiled=True
        ).astype(jnp.float32),
        lax.psum_scatter(
            value_all.astype(jnp.bfloat16), "ctx", scatter_dimension=1, tiled=True
        ).astype(jnp.float32),
    )
    query_grad_low = (query_grad * score_scale).reshape(row_count, head_width).astype(jnp.bfloat16)
    key_grad_low = key_grad.reshape(row_count, head_width).astype(jnp.bfloat16)
    value_grad_low = value_grad.reshape(row_count, head_width).astype(jnp.bfloat16)
    grad_cat = jnp.stack([query_grad_low, key_grad_low, value_grad_low], axis=1)
    qkv_grad = jnp.einsum("td,tcj->dcj", flat_tokens, grad_cat, preferred_element_type=jnp.float32)
    qv_grad = jnp.stack(
        [
            jnp.sum(query_grad_low.astype(jnp.float32), axis=0),
            jnp.sum(value_grad_low.astype(jnp.float32), axis=0),
        ]
    )
    input_part = contract_last(
        grad_cat.reshape(row_count, 3 * head_width), w_qkv.reshape(width, 3 * head_width)
    )
    gains_grad = jnp.stack([gain1_grad, gain2_grad], axis=1)
    shifts_grad = jnp.stack([shift1_grad, shift2_grad], axis=1)
    tokens_full = resid_grad + lax.psum(input_part.astype(jnp.bfloat16), "tp").astype(jnp.float32)
    tokens_share = own_rows(to_three(tokens_full))
    output_share = own_rows(to_three(final_out))
    biases_grad = jnp.stack(
        [out_bias_grad, shifts_grad[:, 0], down_bias_grad, shifts_grad[:, 1]], axis=1
    )
    shards = (
        lax.psum_scatter(qkv_grad, ("fsdp", "ctx"), scatter_dimension=0, tiled=True),
        lax.psum_scatter(out_grad, ("fsdp", "ctx"), scatter_dimension=0, tiled=True),
        lax.psum_scatter(up_grad, ("fsdp", "ctx"), scatter_dimension=0, tiled=True),
        lax.psum_scatter(down_grad, ("fsdp", "ctx"), scatter_dimension=0, tiled=True),
        lax.psum_scatter(gains_grad, ("fsdp", "ctx"), scatter_dimension=0, tiled=True),
        lax.psum_scatter(biases_grad, ("fsdp", "ctx"), scatter_dimension=0, tiled=True),
    )
    qv_total, up_total = lax.psum((qv_grad, up_bias_grad), ("fsdp", "ctx"))
    output = output_share.astype(jnp.bfloat16)
    tokens_out = tokens_share.astype(jnp.bfloat16)
    return (
        output,
        tokens_out,
        shards[0],
        qv_total,
        shards[1],
        shards[2],
        up_total,
        shards[3],
        shards[4],
        shards[5],
    )


def solution(mesh):
    in_specs = (
        P("fsdp", "ctx", None),
        P(("fsdp", "ctx"), None, "tp"),
        P(None, "tp"),
        P(("fsdp", "ctx"), "tp"),
        P(("fsdp", "ctx"), "tp"),
        P("tp"),
        P(("fsdp", "ctx"), "tp"),
        P(("fsdp", "ctx"), None),
        P(("fsdp", "ctx"), None),
        P("fsdp", "ctx", None),
    )
    out_specs = (
        P("fsdp", ("ctx", "tp"), None),
        P("fsdp", ("ctx", "tp"), None),
        P(("fsdp", "ctx"), None, "tp"),
        P(None, "tp"),
        P(("fsdp", "ctx"), "tp"),
        P(("fsdp", "ctx"), "tp"),
        P("tp"),
        P(("fsdp", "ctx"), "tp"),
        P(("fsdp", "ctx"), None),
        P(("fsdp", "ctx"), None),
    )
    return jax.shard_map(body, mesh=mesh, in_specs=in_specs, out_specs=out_specs, check_vma=False)
```

profile of v0, /device:TPU:0, one launch (start us, length us, event | category | flops | bytes accessed | tf_op | source)
XLA Modules:
  0.0 2090.9 jit_solution(9542823779875088038)
XLA Ops:
  8.0 45.5 %all-gather.8.cloned.1.call-done = bf16[768,3,384]{2,0,1:T(8,128)(2,1)} async-done(((bf16[48,3,384]{2,0,1:T(8,128)(2,1)}), bf16[768,3,384]{2,0,1:T(8,128)(2,1)}) %all-gather.8.cloned.1.call-update) | async-done | bytes 1769488 | tf_op jit(solution)/shard_map/all_gather | solution.py:94
  67.9 53.4 %all_gather.27 = bf16[768,384]{1,0:T(8,128)(2,1)} all-gather(bf16[48,384]{1,0:T(8,128)(2,1)S(1)} %copy-done.33), channel_id=1, replica_groups=mesh['fsdp'=4,'ctx'=4,'tp'=2] {'fsdp','ctx'}, dimensions={0}, use_global_device_ids=true | all-gather | bytes 626688 | tf_op jit(solution)/shard_map/all_gather | solution.py:95
  142.1 48.3 %all-gather.12.cloned.1.call-done = bf16[2,4096,384]{1,2,0:T(8,128)(2,1)} async-done(((bf16[2,1024,384]{1,2,0:T(8,128)(2,1)}), bf16[2,4096,384]{1,2,0:T(8,128)(2,1)}) %all-gather.12.cloned.1.call-update) | async-done | bytes 6291472 | tf_op jit(solution)/shard_map/all_gather | solution.py:116
  190.4 93.1 %while.48 = (s32[]{:T(128)}, f32[2,6,1024]{2,1,0:T(8,128)S(1)}, f32[2,6,1024]{2,1,0:T(8,128)S(1)}, bf16[2,4096,384]{1,2,0:T(8,128)(2,1)}, bf16[2,1024,6,64]{1,3,...) while((s32[]{:T(128)}, f32[2,6,1024]{2,1,0:T(8,128)S(1)}, ...), condition=%wide.region_3.0_spmd.clone, body=%wide.region_0.0_spmd.clone.sunk | while | flops 836825088 | bytes 54902944 | solution.py:141
  283.4 22.7 %all-gather.10.cloned.1.call-done = bf16[2,4096,384]{1,2,0:T(8,128)(2,1)} async-done(((bf16[2,1024,384]{1,2,0:T(8,128)(2,1)}), bf16[2,4096,384]{1,2,0:T(8,128)(2,1)}) %all-gather.10.cloned.1.call-update) | async-done | bytes 6291472 | tf_op jit(solution)/shard_map/all_gather | solution.py:119
  306.2 88.7 %while.49 = (s32[]{:T(128)}, f32[2,1024,6,64]{1,3,2,0:T(8,128)}, bf16[2,4096,384]{1,2,0:T(8,128)(2,1)}, bf16[2,4096,384]{1,2,0:T(8,128)(2,1)}, bf16[2,1024,6,64]...) while((s32[]{:T(128)}, f32[2,1024,6,64]{1,3,2,0:T(8,128)}, ...), condition=%wide.region_5.0_spmd.clone, body=%wide.region_4.0_spmd.clone.sunk | while | flops 1637351424 | bytes 12681393 | solution.py:164
  405.1 29.4 %all-gather.1 = bf16[16,48,2]{1,2,0:T(2,128)(2,1)S(1)} all-gather(bf16[1,48,2]{1,2,0:T(2,128)(2,1)S(1)} %bitcast.191), channel_id=1, replica_groups=mesh['fsdp'=4,'ctx'=4,'tp'=2] {'fsdp','ctx'}, dimensions={0}, use_global_device_ids=true | all-gather | bytes 3264 | tf_op jit(solution)/shard_map/all_gather | solution.py:98
  434.7 29.8 %all-gather = bf16[16,48,4]{1,2,0:T(4,128)(2,1)S(1)} all-gather(bf16[1,48,4]{1,2,0:T(4,128)(2,1)S(1)} %bitcast.190), channel_id=1, replica_groups=mesh['fsdp'=4,'ctx'=4,'tp'=2] {'fsdp','ctx'}, dimensions={0}, use_global_device_ids=true | all-gather | bytes 6528 | tf_op jit(solution)/shard_map/all_gather | solution.py:99
  465.2 22.8 %all-reduce.8.cloned.1.call-done = bf16[2048,768]{1,0:T(8,128)(2,1)} async-done(((bf16[2048,768]{1,0:T(8,128)(2,1)}), bf16[2048,768]{1,0:T(8,128)(2,1)}) %all-reduce.8.cloned.1.call-update) | async-done | bytes 3145744 | tf_op jit(solution)/shard_map/psum | solution.py:167
  496.9 35.6 %all-gather.14.cloned.1.call-done = bf16[768,1536]{1,0:T(8,128)(2,1)} async-done(((bf16[48,1536]{1,0:T(8,128)(2,1)}), bf16[768,1536]{1,0:T(8,128)(2,1)}) %all-gather.14.cloned.1.call-update) | async-done | bytes 2359312 | tf_op jit(solution)/shard_map/all_gather | solution.py:96
  532.5 35.1 %multiply_convert_fusion.1 = (bf16[2048,1536]{1,0:T(8,128)(2,1)}, f32[2048,1536]{1,0:T(8,128)}, f32[2048,1536]{1,0:T(8,128)}) fusion(f32[1536]{0:T(1024)S(1)} %convert_element_type.186, bf16[768,1536]{1,0:T(8,128)(2,1)} %all-gather.14.cloned.1.call-done, f32[2048,768]{1,0:T(8,128)} %subtract_multiply_fusion.2, f32[768]{0:T(1024)S(1)} %get-tuple-element.637, ...), kind=kOutput, calls=%fused_computation.29 | convolution fusion | flops 5044174848 | bytes 40120320 | tf_op jit(solution)/shard_map/dot_general | solution.py:172
  587.0 82.7 %all-reduce.10.cloned.1.call-done = bf16[2048,768]{1,0:T(8,128)(2,1)} async-done(((bf16[2048,768]{1,0:T(8,128)(2,1)}), bf16[2048,768]{1,0:T(8,128)(2,1)}) %all-reduce.10.cloned.1.call-update) | async-done | bytes 3145744 | tf_op jit(solution)/shard_map/psum | solution.py:178
  681.4 18.9 convert_reduce_fusion
  709.4 85.9 %all-reduce.12.cloned.1.call-done = bf16[2048,768]{1,0:T(8,128)(2,1)} async-done(((bf16[2048,768]{1,0:T(8,128)(2,1)}), bf16[2048,768]{1,0:T(8,128)(2,1)}) %all-reduce.12.cloned.1.call-update) | async-done | bytes 3145744 | tf_op jit(solution)/shard_map/psum | solution.py:194
  830.2 482.1 %while.50 = (s32[]{:T(128)}, f32[2,1024,6,64]{1,3,2,0:T(8,128)}, bf16[2,4096,384]{1,2,0:T(8,128)(2,1)}, bf16[2,4096,384]{1,2,0:T(8,128)(2,1)}, bf16[2,4096,384]{...) while((s32[]{:T(128)}, f32[2,1024,6,64]{1,3,2,0:T(8,128)}, ...), condition=%wide.region_18.0_spmd.clone, body=%wide.region_17.0_spmd.clone.sunk | while | flops 4072931328 | bytes 139346160 | solution.py:237
  856.5 14.5 multiply_convert_fusion.5
  915.8 14.5 multiply_convert_fusion.5
  976.1 14.5 multiply_convert_fusion.5
  1036.4 14.5 multiply_convert_fusion.5
  1096.7 14.5 multiply_convert_fusion.5
  1157.1 14.5 multiply_convert_fusion.5
  1217.5 14.5 multiply_convert_fusion.5
  1277.9 14.5 multiply_convert_fusion.5
  1328.0 95.3 %reduce-scatter.12.cloned.1.call-done = bf16[2,1024,384]{1,2,0:T(8,128)(2,1)} async-done(((bf16[2,4096,384]{1,2,0:T(8,128)(2,1)}), bf16[2,1024,384]{1,2,0:T(8,128)(2,1)}) %reduce-scatter.12.cloned.1.call-update) | async-done | bytes 1572880 | tf_op jit(solution)/shard_map/reduce_scatter | solution.py:241
  1425.9 110.9 %reduce-scatter.14.cloned.1.call-done = bf16[2,1024,384]{1,2,0:T(8,128)(2,1)} async-done(((bf16[2,4096,384]{1,2,0:T(8,128)(2,1)}), bf16[2,1024,384]{1,2,0:T(8,128)(2,1)}) %reduce-scatter.14.cloned.1.call-update) | async-done | bytes 1572880 | tf_op jit(solution)/shard_map/reduce_scatter | solution.py:244
  1598.2 57.1 %reduce-scatter.24.cloned.1.call-done = f32[48,4]{1,0:T(8,128)} async-done(((f32[768,4]{1,0:T(8,128)}), f32[48,4]{1,0:T(8,128)}) %reduce-scatter.24.cloned.1.call-update) | async-done | bytes 784
  1656.9 61.1 %all-reduce.1 = (f32[2,384]{1,0:T(2,128)}, f32[1536]{0:T(1024)}) all-reduce(f32[2,384]{1,0:T(2,128)S(1)} %pad_maximum_fusion.5, f32[1536]{0:T(1024)S(1)} %copy-done.43), channel_id=1, replica_groups=mesh['fsdp'=4,'ctx'=4,'tp'=2] {'fsdp','ctx'}, use_global_device_ids=true, to_apply=%region_25.0 | all-reduce | flops 2304 | bytes 18432 | tf_op jit(solution)/shard_map/psum | solution.py:278
  1718.1 58.1 %all-reduce.16.cloned.1.call-done = f32[768,3,384]{2,1,0:T(4,128)} async-done(((f32[768,3,384]{2,1,0:T(4,128)}), f32[768,3,384]{2,1,0:T(4,128)}) %all-reduce.16.cloned.1.call-update) | async-done | bytes 3538960
  1777.8 86.1 %all-reduce.14.cloned.1.call-done = bf16[2048,768]{1,0:T(8,128)(2,1)} async-done(((bf16[2048,768]{1,0:T(8,128)(2,1)}), bf16[2048,768]{1,0:T(8,128)(2,1)}) %all-reduce.14.cloned.1.call-update) | async-done | bytes 3145744 | tf_op jit(solution)/shard_map/psum | solution.py:264
  1869.6 56.6 %reduce-scatter.16.cloned.1.call-done = f32[48,384]{1,0:T(8,128)} async-done(((f32[768,384]{1,0:T(8,128)}), f32[48,384]{1,0:T(8,128)}) %reduce-scatter.16.cloned.1.call-update) | async-done | bytes 73744 | tf_op jit(solution)/shard_map/reduce_scatter | solution.py:272
  1926.2 78.9 %reduce-scatter.20.cloned.1.call-done = f32[48,1536]{1,0:T(8,128)} async-done(((f32[768,1536]{1,0:T(8,128)}), f32[48,1536]{1,0:T(8,128)}) %reduce-scatter.20.cloned.1.call-update) | async-done | bytes 294928 | tf_op jit(solution)/shard_map/reduce_scatter | solution.py:274
  2005.0 79.2 %reduce-scatter.18.cloned.1.call-done = f32[48,1536]{1,0:T(8,128)} async-done(((f32[768,1536]{1,0:T(8,128)}), f32[48,1536]{1,0:T(8,128)}) %reduce-scatter.18.cloned.1.call-update) | async-done | bytes 294928 | tf_op jit(solution)/shard_map/reduce_scatter | solution.py:273
  (360 shorter events, 764.9 us)
Async XLA Ops:
  7.2 46.2 %all-gather.8.cloned.1.call-start = ((), (), s32[]{:S(2)}) async-start(), calls=%async_computation.7 | async-start | bytes 1880064 | tf_op jit(solution)/shard_map/all_gather | solution.py:94
  7.9 182.5 %all-gather.12.cloned.1.call-start = ((), (), s32[]{:S(2)}) async-start(), calls=%async_computation.9 | async-start | bytes 7864320 | tf_op jit(solution)/shard_map/all_gather | solution.py:116
  67.7 238.5 %all-gather.10.cloned.1.call-start = ((), (), s32[]{:S(2)}) async-start(), calls=%async_computation.8 | async-start | bytes 7864320 | tf_op jit(solution)/shard_map/all_gather | solution.py:119
  141.9 346.1 %all-reduce.8.cloned.1.call-start = ((), (), s32[]{:S(2)}) async-start(), calls=%async_computation.10 | async-start | bytes 6291456 | tf_op jit(solution)/shard_map/psum | solution.py:167
  400.4 34.3 %copy-start.46 = (bf16[48,4]{0,1:T(4,128)(2,1)S(1)}, bf16[48,4]{0,1:T(4,128)(2,1)}, u32[]{:S(2)}) copy-start(bf16[48,4]{0,1:T(4,128)(2,1)} %param.24) | copy-start | bytes 1156
  400.4 87.7 %copy-start.7 = (bf16[2,1024,768]{2,1,0:T(8,128)(2,1)S(1)}, bf16[2,1024,768]{2,1,0:T(8,128)(2,1)}, u32[]{:S(2)}) copy-start(bf16[2,1024,768]{2,1,0:T(8,128)(2,1)} %param.16) | copy-start | bytes 9437188
  403.9 128.7 %all-gather.14.cloned.1.call-start = ((), (), s32[]{:S(2)}) async-start(), calls=%async_computation.11 | async-start | bytes 2506752 | tf_op jit(solution)/shard_map/all_gather | solution.py:96
  404.4 171.3 %all-gather.16.cloned.1.call-start = ((), (), s32[]{:S(2)}) async-start(), calls=%async_computation.12 | async-start | bytes 2506752 | tf_op jit(solution)/shard_map/all_gather | solution.py:97
  405.0 264.7 %all-reduce.10.cloned.1.call-start = ((), (), s32[]{:S(2)}) async-start(), calls=%async_computation.13 | async-start | bytes 6291456 | tf_op jit(solution)/shard_map/psum | solution.py:178
  434.6 244.5 %copy-start.27 = (f32[768]{0:T(1024)}, f32[768]{0:T(1024)S(1)}, u32[]{:S(2)}) copy-start(f32[768]{0:T(1024)S(1)} %get-tuple-element.639) | copy-start | bytes 9220
  434.7 370.4 %copy-start.31 = (f32[768]{0:T(1024)}, f32[768]{0:T(1024)S(1)}, u32[]{:S(2)}) copy-start(f32[768]{0:T(1024)S(1)} %get-tuple-element.640) | copy-start | bytes 9220
  465.2 204.5 %copy-start.35 = (f32[768]{0:T(1024)}, f32[768]{0:T(1024)S(1)}, u32[]{:S(2)}) copy-start(f32[768]{0:T(1024)S(1)} %get-tuple-element.637) | copy-start | bytes 9220
  585.0 210.3 %all-reduce.12.cloned.1.call-start = ((), (), s32[]{:S(2)}) async-start(), calls=%async_computation.14 | async-start | bytes 6291456 | tf_op jit(solution)/shard_map/psum | solution.py:194
  681.4 18.9 copy-start.4
  709.3 713.9 %reduce-scatter.12.cloned.1.call-start = ((), (), s32[]{:S(2)}) async-start(), calls=%async_computation.15 | async-start | bytes 7864320 | tf_op jit(solution)/shard_map/reduce_scatter | solution.py:241
  709.4 95.6 %copy-start.30 = (f32[2048]{0:T(1024)S(1)}, f32[2048]{0:T(1024)}, u32[]{:S(2)}) copy-start(f32[2048]{0:T(1024)} %copy-done.29) | copy-start | bytes 24580
  1312.3 224.4 %reduce-scatter.14.cloned.1.call-start = ((), (), s32[]{:S(2)}) async-start(), calls=%async_computation.16 | async-start | bytes 7864320 | tf_op jit(solution)/shard_map/reduce_scatter | solution.py:244
  1312.9 283.8 %reduce-scatter.22.cloned.1.call-start = ((), (), s32[]{:S(2)}) async-start(), calls=%async_computation.21 | async-start | bytes 417792
  1315.6 339.6 %reduce-scatter.24.cloned.1.call-start = ((), (), s32[]{:S(2)}) async-start(), calls=%async_computation.22 | async-start | bytes 417792
  1321.4 217.9 %copy-start.8 = (bf16[2,1024,768]{2,1,0:T(8,128)(2,1)S(1)}, bf16[2,1024,768]{2,1,0:T(8,128)(2,1)}, u32[]{:S(2)}) copy-start(bf16[2,1024,768]{2,1,0:T(8,128)(2,1)} %param.16) | copy-start | bytes 9437188
  1327.9 448.2 %all-reduce.16.cloned.1.call-start = ((), (), s32[]{:S(2)}) async-start(), calls=%async_computation.23 | async-start | bytes 9437184
  1553.8 310.0 %all-reduce.14.cloned.1.call-start = ((), (), s32[]{:S(2)}) async-start(), calls=%async_computation.17 | async-start | bytes 6291456 | tf_op jit(solution)/shard_map/psum | solution.py:264
  1562.5 363.6 %reduce-scatter.16.cloned.1.call-start = ((), (), s32[]{:S(2)}) async-start(), calls=%async_computation.18 | async-start | bytes 1253376 | tf_op jit(solution)/shard_map/reduce_scatter | solution.py:272
  1568.4 436.6 %reduce-scatter.20.cloned.1.call-start = ((), (), s32[]{:S(2)}) async-start(), calls=%async_computation.20 | async-start | bytes 5013504 | tf_op jit(solution)/shard_map/reduce_scatter | solution.py:274
  1579.0 10.7 copy-start.48
  1579.0 11.9 copy-start.24
  1579.0 11.9 copy-start.26
  1579.0 11.9 copy-start.28
  1579.0 11.9 copy-start.34
  1579.0 505.2 %reduce-scatter.18.cloned.1.call-start = ((), (), s32[]{:S(2)}) async-start(), calls=%async_computation.19 | async-start | bytes 5013504 | tf_op jit(solution)/shard_map/reduce_scatter | solution.py:273
  1590.9 65.7 %copy-start.15 = (bf16[2,1024,384]{1,2,0:T(8,128)(2,1)S(1)}, bf16[2,1024,384]{1,2,0:T(8,128)(2,1)}, u32[]{:S(2)}) copy-start(bf16[2,1024,384]{1,2,0:T(8,128)(2,1)} %reduce-scatter.14.cloned.1.call-done) | copy-start | bytes 4718596
  1590.9 66.0 %copy-start.43 = (f32[1536]{0:T(1024)S(1)}, f32[1536]{0:T(1024)}, u32[]{:S(2)}) copy-start(f32[1536]{0:T(1024)} %get-tuple-element.708) | copy-start | bytes 18436
  (41 other events, 230.5 us)
Sparse Core Ops, SparseCore 0:
  10.2 43.1 all-gather.7
  67.8 122.5 all-gather.11
  192.5 113.6 all-gather.9
  404.0 83.9 all-reduce.7
  490.2 42.3 all-gather.13
  534.7 41.0 all-gather.15
  585.1 84.5 all-reduce.9
  709.5 85.8 all-reduce.11
  1312.5 110.7 reduce-scatter.11
  1425.4 111.2 reduce-scatter.13
  1540.2 56.4 reduce-scatter.21
  1600.1 55.0 reduce-scatter.23
  1658.8 117.2 all-reduce.15
  1778.3 85.5 all-reduce.13
  1867.9 58.1 reduce-scatter.15
  1930.4 74.5 reduce-scatter.19
  2009.3 74.8 reduce-scatter.17
where the time goes:
time: 2100 us; the launch traced here: 2090 us
  waiting for transfers between devices  977 us (47%)
  matrix products  697 us (33%)
  blocking collectives  174 us (8%)
  local copies, waits for them, and re-layouts  134 us (6%)
  other arithmetic  92 us (4%)
    dot_general x16, matrix products, block_scores(): jnp.einsum('sqhd,skhd->shqk', query_four, key_four, preferred_element_typ...  141 us
    unnamed x20, waiting for transfers between devices  119 us
    dot_general x8, matrix products, score_grads(): jnp.einsum('sqhd,skhd->shqk', grad_four, value_four, preferred_element_ty...  116 us
    reduce_scatter x1, waiting for transfers between devices, body(): lax.psum_scatter(value_all.astype(jnp.bfloat16), 'ctx', scatter_dimension...  111 us
    reduce_scatter x1, waiting for transfers between devices, body(): lax.psum_scatter(key_all.astype(jnp.bfloat16), 'ctx', scatter_dimension=1...  95.3 us
    dot_general x8, matrix products, grad_step(): jnp.einsum('shqk,sqhd->skhd', prob_low, grad_four, preferred_element_type...  89.2 us
    psum x1, waiting for transfers between devices, body(): lax.psum(input_part.astype(jnp.bfloat16), 'tp').astype(jnp.float32)  86.1 us
    psum x1, waiting for transfers between devices, body(): lax.psum(back_part.astype(jnp.bfloat16), 'tp').astype(jnp.float32)  85.9 us
  transfers between devices with their start and end apart: 17, of which 17 were waited for; matrix products, arithmetic and copies ran while one was open for 12% of the time, Pallas kernels for 0%

commit v1 on v0

--- a/solution.py
+++ b/solution.py
@@ -7,6 +7,28 @@
 epsilon = 1e-12
 score_scale = 0.125
 highest = lax.Precision.HIGHEST
+
+
+def laid_out(tiles, dim):
+    dims = list(tiles.shape[1:])
+    dims[dim] *= tiles.shape[0]
+    return jnp.moveaxis(tiles, 0, dim).reshape(dims)
+
+
+def collect(array, axis, dim):
+    length = lax.axis_size(axis)
+    pairs = [(i, (i + 1) % length) for i in range(length)]
+    back = [(b, a) for a, b in pairs]
+    lower, upper = ([], [])
+    for step in range(length - 1):
+        if step % 2 == 0:
+            lower.append(lax.ppermute(lower[-1] if lower else array, axis, pairs))
+        else:
+            upper.append(lax.ppermute(upper[-1] if upper else array, axis, back))
+    blocks = jnp.stack([*lower[::-1], array, *upper])
+    shift = lax.axis_index(axis) - len(lower)
+    blocks = blocks[(jnp.arange(length) - shift) % length]
+    return laid_out(blocks, dim)
 
 
 def contract_last(left, right):
@@ -91,7 +113,7 @@
         return array_two.reshape(seq_count, array_two.shape[0] // seq_count, array_two.shape[1])
 
     gathered = (
-        lax.all_gather(qkv_weight, ("fsdp", "ctx"), axis=0, tiled=True),
+        collect(qkv_weight, ("fsdp", "ctx"), 0),
         lax.all_gather(out_weight, ("fsdp", "ctx"), axis=0, tiled=True),
         lax.all_gather(up_weight, ("fsdp", "ctx"), axis=0, tiled=True),
         lax.all_gather(down_weight, ("fsdp", "ctx"), axis=0, tiled=True),

time: 2100 us -> 1960 us (0.933)
  waiting for transfers between devices: 977 us -> 696 us
  other arithmetic: 92 us -> 143 us
  starting transfers between devices: 1.44 us -> 34.8 us
  local copies, waits for them, and re-layouts: 134 us -> 163 us
  matrix products: 697 us -> 725 us
    reduce_scatter x1, waiting for transfers between devices: 56.6 us -> 0.01 us  [body(): lax.psum_scatter(out_grad, ('fsdp', 'ctx'), scatter_dimension=0, tiled=True)]
    unnamed x20 -> x19, waiting for transfers between devices: 119 us -> 62.1 us
    reduce_sum x8, other arithmetic: 34.4 us -> 83.8 us  [stats_step(): jnp.sum(jnp.exp(scores - new_max[..., None]), axis=-1)]
    reduce_scatter x1, waiting for transfers between devices: 78.9 us -> 31.9 us  [body(): lax.psum_scatter(down_grad, ('fsdp', 'ctx'), scatter_dimension=0, tiled=T...]
    psum x1, waiting for transfers between devices: 86.1 us -> 39.4 us  [body(): lax.psum(input_part.astype(jnp.bfloat16), 'tp').astype(jnp.float32)]
    all_gather x1 -> x0, waiting for transfers between devices: 45.5 us -> none  [body(): lax.all_gather(qkv_weight, ('fsdp', 'ctx'), axis=0, tiled=True)]
    dot_general x16, matrix products: 141 us -> 181 us  [block_scores(): jnp.einsum('sqhd,skhd->shqk', query_four, key_four, preferred_element_typ...]
    unnamed x107 -> x135, local copies, waits for them, and re-layouts: 17.4 us -> 54.3 us
  transfers between devices with their start and end apart: 17 -> 31, of which waited for: 17 -> 21; matrix products, arithmetic and copies ran while one was open for 12% -> 18% of each run, Pallas kernels for 0% -> 0%
where the time goes in v1:
time: 1960 us; the launch traced here: 1950 us
  matrix products  725 us (37%)
  waiting for transfers between devices  696 us (36%)
  blocking collectives  170 us (9%)
  local copies, waits for them, and re-layouts  163 us (8%)
  other arithmetic  143 us (7%)
  starting transfers between devices  34.8 us (2%)
    dot_general x16, matrix products, block_scores(): jnp.einsum('sqhd,skhd->shqk', query_four, key_four, preferred_element_typ...  181 us
    dot_general x8, matrix products, score_grads(): jnp.einsum('sqhd,skhd->shqk', grad_four, value_four, preferred_element_ty...  116 us
    reduce_scatter x1, waiting for transfers between devices, body(): lax.psum_scatter(value_all.astype(jnp.bfloat16), 'ctx', scatter_dimension...  108 us
    reduce_scatter x1, waiting for transfers between devices, body(): lax.psum_scatter(key_all.astype(jnp.bfloat16), 'ctx', scatter_dimension=1...  103 us
    psum x1, waiting for transfers between devices, body(): lax.psum(back_part.astype(jnp.bfloat16), 'tp').astype(jnp.float32)  85.7 us
    reduce_sum x8, other arithmetic, stats_step(): jnp.sum(jnp.exp(scores - new_max[..., None]), axis=-1)  83.8 us
    psum x1, waiting for transfers between devices, body(): lax.psum(ffn_part.astype(jnp.bfloat16), 'tp').astype(jnp.float32)  83.5 us
    dot_general x8, matrix products, grad_step(): jnp.einsum('shqk,sqhd->skhd', prob_low, grad_four, preferred_element_type...  82.4 us
  transfers between devices with their start and end apart: 31, of which 21 were waited for; matrix products, arithmetic and copies ran while one was open for 18% of the time, Pallas kernels for 0%

profile of v1, /device:TPU:0, one launch (start us, length us, event | category | flops | bytes accessed | tf_op | source)
XLA Modules:
  0.0 1950.7 jit_solution(18260021035707292565)
XLA Ops:
  96.0 48.8 %all_gather.23 = bf16[768,384]{1,0:T(8,128)(2,1)} all-gather(bf16[48,384]{1,0:T(8,128)(2,1)S(1)} %copy-done.35), channel_id=1, replica_groups=mesh['fsdp'=4,'ctx'=4,'tp'=2] {'fsdp','ctx'}, dimensions={0}, use_global_device_ids=true | all-gather | bytes 626688 | tf_op jit(solution)/shard_map/all_gather | solution.py:117
  164.1 52.5 %all-gather.9.cloned.1.call-done = bf16[2,4096,384]{2,1,0:T(8,128)(2,1)} async-done(((bf16[2,1024,384]{2,1,0:T(8,128)(2,1)}), bf16[2,4096,384]{2,1,0:T(8,128)(2,1)}) %all-gather.9.cloned.1.call-update) | async-done | bytes 6291472 | tf_op jit(solution)/shard_map/all_gather | solution.py:138
  225.2 175.3 %while.48 = (s32[]{:T(128)}, f32[2,6,1024]{2,1,0:T(8,128)S(1)}, f32[2,6,1024]{2,1,0:T(8,128)S(1)}, bf16[2,4096,384]{1,2,0:T(8,128)(2,1)}, bf16[2,1024,6,64]{1,3,...) while((s32[]{:T(128)}, f32[2,6,1024]{2,1,0:T(8,128)S(1)}, ...), condition=%wide.region_3.4_spmd.clone, body=%wide.region_0.3_spmd.clone.sunk | while | flops 836825088 | bytes 54902936 | solution.py:163
  409.4 85.8 %while.49 = (s32[]{:T(128)}, f32[2,1024,6,64]{1,3,2,0:T(8,128)}, bf16[2,4096,384]{1,2,0:T(8,128)(2,1)}, bf16[2,4096,384]{1,2,0:T(8,128)(2,1)}, bf16[2,1024,6,64]...) while((s32[]{:T(128)}, f32[2,1024,6,64]{1,3,2,0:T(8,128)}, ...), condition=%wide.region_5.6_spmd.clone, body=%wide.region_4.5_spmd.clone.sunk | while | flops 1637351424 | bytes 12681385 | solution.py:186
  506.0 30.9 %all-gather = bf16[16,48,4]{1,2,0:T(4,128)(2,1)S(1)} all-gather(bf16[1,48,4]{1,2,0:T(4,128)(2,1)S(1)} %bitcast.229), channel_id=1, replica_groups=mesh['fsdp'=4,'ctx'=4,'tp'=2] {'fsdp','ctx'}, dimensions={0}, use_global_device_ids=true | all-gather | bytes 6528 | tf_op jit(solution)/shard_map/all_gather | solution.py:121
  537.6 28.7 %all-gather.1 = bf16[16,48,2]{1,2,0:T(2,128)(2,1)S(1)} all-gather(bf16[1,48,2]{1,2,0:T(2,128)(2,1)S(1)} %bitcast.230), channel_id=1, replica_groups=mesh['fsdp'=4,'ctx'=4,'tp'=2] {'fsdp','ctx'}, dimensions={0}, use_global_device_ids=true | all-gather | bytes 3264 | tf_op jit(solution)/shard_map/all_gather | solution.py:120
  566.5 23.5 %all-reduce.8.cloned.1.call-done = bf16[2048,768]{1,0:T(8,128)(2,1)} async-done(((bf16[2048,768]{1,0:T(8,128)(2,1)}), bf16[2048,768]{1,0:T(8,128)(2,1)}) %all-reduce.8.cloned.1.call-update) | async-done | bytes 3145744 | tf_op jit(solution)/shard_map/psum | solution.py:189
  600.3 35.1 %multiply_convert_fusion.1 = (bf16[2048,1536]{1,0:T(8,128)(2,1)}, f32[2048,1536]{1,0:T(8,128)}, f32[2048,1536]{1,0:T(8,128)}) fusion(f32[1536]{0:T(1024)S(1)} %convert_element_type.186, bf16[768,1536]{1,0:T(8,128)(2,1)} %all-gather.11.cloned.1.call-done, f32[2048,768]{1,0:T(8,128)} %subtract_multiply_fusion.2, f32[768]{0:T(1024)S(1)} %get-tuple-element.637, ...), kind=kOutput, calls=%fused_computation.30 | convolution fusion | flops 5044174848 | bytes 40120320 | tf_op jit(solution)/shard_map/dot_general | solution.py:194
  647.0 83.5 %all-reduce.10.cloned.1.call-done = bf16[2048,768]{1,0:T(8,128)(2,1)} async-done(((bf16[2048,768]{1,0:T(8,128)(2,1)}), bf16[2048,768]{1,0:T(8,128)(2,1)}) %all-reduce.10.cloned.1.call-update) | async-done | bytes 3145744 | tf_op jit(solution)/shard_map/psum | solution.py:200
  741.9 18.8 convert_reduce_fusion
  770.1 85.7 %all-reduce.12.cloned.1.call-done = bf16[2048,768]{1,0:T(8,128)(2,1)} async-done(((bf16[2048,768]{1,0:T(8,128)(2,1)}), bf16[2048,768]{1,0:T(8,128)(2,1)}) %all-reduce.12.cloned.1.call-update) | async-done | bytes 3145744 | tf_op jit(solution)/shard_map/psum | solution.py:216
  890.5 474.8 %while.50 = (s32[]{:T(128)}, f32[2,1024,6,64]{1,3,2,0:T(8,128)}, bf16[2,4096,384]{1,2,0:T(8,128)(2,1)}, bf16[2,4096,384]{1,2,0:T(8,128)(2,1)}, bf16[2,4096,384]{...) while((s32[]{:T(128)}, f32[2,1024,6,64]{1,3,2,0:T(8,128)}, ...), condition=%wide.region_18.19_spmd.clone, body=%wide.region_17.18_spmd.clone.sunk | while | flops 4072931328 | bytes 136200400 | solution.py:259
  891.9 12.5 exponential_divide_fusion.2
  905.6 14.5 multiply_convert_fusion.5
  950.3 12.6 exponential_divide_fusion.2
  964.1 14.5 multiply_convert_fusion.5
  1009.8 12.6 exponential_divide_fusion.2
  1023.5 14.5 multiply_convert_fusion.5
  1082.9 14.5 multiply_convert_fusion.5
  1128.6 12.6 exponential_divide_fusion.2
  1142.3 14.5 multiply_convert_fusion.5
  1188.0 12.5 exponential_divide_fusion.2
  1201.7 14.5 multiply_convert_fusion.5
  1261.3 14.5 multiply_convert_fusion.5
  1320.7 14.5 multiply_convert_fusion.5
  1373.2 103.0 %reduce-scatter.12.cloned.1.call-done = bf16[2,1024,384]{1,2,0:T(8,128)(2,1)} async-done(((bf16[2,4096,384]{1,2,0:T(8,128)(2,1)}), bf16[2,1024,384]{1,2,0:T(8,128)(2,1)}) %reduce-scatter.12.cloned.1.call-update) | async-done | bytes 1572880 | tf_op jit(solution)/shard_map/reduce_scatter | solution.py:263
  1481.7 108.2 %reduce-scatter.14.cloned.1.call-done = bf16[2,1024,384]{1,2,0:T(8,128)(2,1)} async-done(((bf16[2,4096,384]{1,2,0:T(8,128)(2,1)}), bf16[2,1024,384]{1,2,0:T(8,128)(2,1)}) %reduce-scatter.14.cloned.1.call-update) | async-done | bytes 1572880 | tf_op jit(solution)/shard_map/reduce_scatter | solution.py:266
  1661.4 60.2 %reduce-scatter.24.cloned.1.call-done = f32[48,4]{1,0:T(8,128)} async-done(((f32[768,4]{1,0:T(8,128)}), f32[48,4]{1,0:T(8,128)}) %reduce-scatter.24.cloned.1.call-update) | async-done | bytes 784
  1723.2 61.8 %all-reduce.1 = (f32[2,384]{1,0:T(2,128)}, f32[1536]{0:T(1024)}) all-reduce(f32[2,384]{1,0:T(2,128)S(1)} %pad_maximum_fusion.2, f32[1536]{0:T(1024)S(1)} %copy-done.45), channel_id=1, replica_groups=mesh['fsdp'=4,'ctx'=4,'tp'=2] {'fsdp','ctx'}, use_global_device_ids=true, to_apply=%region_25.26 | all-reduce | flops 2304 | bytes 18432 | tf_op jit(solution)/shard_map/psum | solution.py:300
  1786.8 39.4 %all-reduce.14.cloned.1.call-done = bf16[2048,768]{1,0:T(8,128)(2,1)} async-done(((bf16[2048,768]{1,0:T(8,128)(2,1)}), bf16[2048,768]{1,0:T(8,128)(2,1)}) %all-reduce.14.cloned.1.call-update) | async-done | bytes 3145744 | tf_op jit(solution)/shard_map/psum | solution.py:286
  1831.9 31.9 %reduce-scatter.20.cloned.1.call-done = f32[48,1536]{1,0:T(8,128)} async-done(((f32[768,1536]{1,0:T(8,128)}), f32[48,1536]{1,0:T(8,128)}) %reduce-scatter.20.cloned.1.call-update) | async-done | bytes 294928 | tf_op jit(solution)/shard_map/reduce_scatter | solution.py:296
  1863.8 79.1 %reduce-scatter.18.cloned.1.call-done = f32[48,1536]{1,0:T(8,128)} async-done(((f32[768,1536]{1,0:T(8,128)}), f32[48,1536]{1,0:T(8,128)}) %reduce-scatter.18.cloned.1.call-update) | async-done | bytes 294928 | tf_op jit(solution)/shard_map/reduce_scatter | solution.py:295
  (402 shorter events, 861.9 us)
Async XLA Ops:
  8.0 208.6 %all-gather.9.cloned.1.call-start = ((), (), s32[]{:S(2)}) async-start(), calls=%async_computation.8 | async-start | bytes 7864320 | tf_op jit(solution)/shard_map/all_gather | solution.py:138
  8.1 8.5 collective-permute-start
  16.5 7.9 collective-permute-start.1
  16.5 7.9 collective-permute-start.8
  24.4 8.1 collective-permute-start.2
  24.4 8.1 collective-permute-start.9
  32.5 8.1 collective-permute-start.3
  32.6 8.1 collective-permute-start.10
  40.6 7.0 collective-permute-start.4
  40.7 7.8 collective-permute-start.11
  47.6 7.0 collective-permute-start.5
  48.4 8.0 collective-permute-start.12
  54.6 7.0 collective-permute-start.6
  56.4 7.0 collective-permute-start.13
  61.6 6.9 collective-permute-start.7
  63.4 15.8 collective-permute-start.14
  95.8 304.8 %all-gather.7.cloned.1.call-start = ((), (), s32[]{:S(2)}) async-start(), calls=%async_computation.7 | async-start | bytes 7864320 | tf_op jit(solution)/shard_map/all_gather | solution.py:141
  164.0 426.0 %all-reduce.8.cloned.1.call-start = ((), (), s32[]{:S(2)}) async-start(), calls=%async_computation.9 | async-start | bytes 6291456 | tf_op jit(solution)/shard_map/psum | solution.py:189
  504.8 95.5 %all-gather.11.cloned.1.call-start = ((), (), s32[]{:S(2)}) async-start(), calls=%async_computation.10 | async-start | bytes 2506752 | tf_op jit(solution)/shard_map/all_gather | solution.py:118
  505.3 130.1 %all-gather.13.cloned.1.call-start = ((), (), s32[]{:S(2)}) async-start(), calls=%async_computation.11 | async-start | bytes 2506752 | tf_op jit(solution)/shard_map/all_gather | solution.py:119
  505.9 224.6 %all-reduce.10.cloned.1.call-start = ((), (), s32[]{:S(2)}) async-start(), calls=%async_computation.12 | async-start | bytes 6291456 | tf_op jit(solution)/shard_map/psum | solution.py:200
  566.5 298.7 %copy-start.33 = (f32[768]{0:T(1024)}, f32[768]{0:T(1024)S(1)}, u32[]{:S(2)}) copy-start(f32[768]{0:T(1024)S(1)} %get-tuple-element.640) | copy-start | bytes 9220
  644.6 211.2 %all-reduce.12.cloned.1.call-start = ((), (), s32[]{:S(2)}) async-start(), calls=%async_computation.13 | async-start | bytes 6291456 | tf_op jit(solution)/shard_map/psum | solution.py:216
  769.9 706.4 %reduce-scatter.12.cloned.1.call-start = ((), (), s32[]{:S(2)}) async-start(), calls=%async_computation.14 | async-start | bytes 7864320 | tf_op jit(solution)/shard_map/reduce_scatter | solution.py:263
  1365.3 224.6 %reduce-scatter.14.cloned.1.call-start = ((), (), s32[]{:S(2)}) async-start(), calls=%async_computation.15 | async-start | bytes 7864320 | tf_op jit(solution)/shard_map/reduce_scatter | solution.py:266
  1366.1 293.9 %reduce-scatter.22.cloned.1.call-start = ((), (), s32[]{:S(2)}) async-start(), calls=%async_computation.20 | async-start | bytes 417792
  1372.1 349.4 %reduce-scatter.24.cloned.1.call-start = ((), (), s32[]{:S(2)}) async-start(), calls=%async_computation.21 | async-start | bytes 417792
  1373.2 411.9 %all-reduce.16.cloned.1.call-start = ((), (), s32[]{:S(2)}) async-start(), calls=%async_computation.22 | async-start | bytes 9437184
  1617.8 208.4 %all-reduce.14.cloned.1.call-start = ((), (), s32[]{:S(2)}) async-start(), calls=%async_computation.16 | async-start | bytes 6291456 | tf_op jit(solution)/shard_map/psum | solution.py:286
  1626.4 205.4 %reduce-scatter.16.cloned.1.call-start = ((), (), s32[]{:S(2)}) async-start(), calls=%async_computation.17 | async-start | bytes 1253376 | tf_op jit(solution)/shard_map/reduce_scatter | solution.py:294
  1632.3 231.5 %reduce-scatter.20.cloned.1.call-start = ((), (), s32[]{:S(2)}) async-start(), calls=%async_computation.19 | async-start | bytes 5013504 | tf_op jit(solution)/shard_map/reduce_scatter | solution.py:296
  1643.0 299.9 %reduce-scatter.18.cloned.1.call-start = ((), (), s32[]{:S(2)}) async-start(), calls=%async_computation.18 | async-start | bytes 5013504 | tf_op jit(solution)/shard_map/reduce_scatter | solution.py:295
  (50 other events, 1168.3 us)
Sparse Core Ops, SparseCore 0:
  95.9 120.6 all-gather.8
  218.7 114.4 all-gather.6
  504.9 85.1 all-reduce.7
  644.7 85.7 all-reduce.9
  770.0 85.8 all-reduce.11
  1365.4 110.7 reduce-scatter.11
  1478.5 111.2 reduce-scatter.13
  1593.4 64.2 reduce-scatter.21
  1661.2 60.2 reduce-scatter.23
  1725.6 59.0 reduce-scatter.15
  1789.1 74.6 reduce-scatter.19
  1868.1 74.7 reduce-scatter.17
Sparse Core Ops, SparseCore 1:
  507.5 41.7 all-gather.10
  551.4 40.9 all-gather.12
  1617.9 120.2 all-reduce.15
  1740.4 85.7 all-reduce.13
